TPU v7x, 32 devices: a whole 2x2x4 slice. The times are simulated.
32 devices in a mesh: groups: 2 (over x), expert: 16 (over z, y, core).
Axes of the slice: x: 2, y: 2, z: 4, core: 2. Of those that a mesh axis runs over, the one named last changes fastest.
Arguments:
- tokens: bfloat16 [2048, 2048], P(('groups', 'expert')), parts along dimension 0, may hold values from -6 to 6
- expert_ids: int32 [2048, 8], P(('groups', 'expert')), parts along dimension 0, may hold values from 0 to 15, as said below
- gate_weights: float32 [2048, 8], P(('groups', 'expert')), parts along dimension 0, may hold values from 0.05 to 0.5
- w_gate: bfloat16 [16, 2048, 768], P('expert'), may hold values from -0.125 to 0.125
- w_up: bfloat16 [16, 2048, 768], P('expert'), may hold values from -0.125 to 0.125
- w_down: bfloat16 [16, 768, 2048], P('expert'), may hold values from -0.21875 to 0.21875
Outputs:
- mixed: bfloat16 [2048, 2048], P(('groups', 'expert')), parts along dimension 0
There are 2 independent parts, one for each index of `groups`. A program takes and returns all parts, laid end to end along the dimension named above; an argument that names none is the same for every part. Nothing has to cross between parts.
Inputs may be any that keep to these rules, and one draw needn't show every extreme that they name: `expert_ids`: each token names 8 different experts. Exactly 2 experts are named exactly 64 times by the tokens of every device; every other expert is named at most 28 times by the tokens of one device, and in every draw some such expert is named exactly 28 times by the tokens of every device.
All inputs are finite; a program needn't handle non-finite values.
Results may differ from a plain program's by a relative error of at most 0.0057.
Values may be sent and summed in bfloat16 or wider, within the bound.
A program may use at most 128 MiB of HBM per device.

v0:
```python
import jax
import jax.numpy as jnp
from jax import lax
from jax.sharding import PartitionSpec as P

row_block = 256


def swiglu_rows(rows_in, weights):
    gate_part = jnp.dot(rows_in, weights[0], preferred_element_type=jnp.float32)
    up_part = jnp.dot(rows_in, weights[1], preferred_element_type=jnp.float32)
    hidden = (jax.nn.silu(gate_part) * up_part).astype(jnp.bfloat16)
    return jnp.dot(hidden, weights[2], preferred_element_type=jnp.float32).astype(jnp.bfloat16)


def run_blocks(source_rows, block_total, weights, results):

    def block_step(block_num, current):
        row_start = block_num * row_block
        rows_in = lax.dynamic_slice_in_dim(source_rows, row_start, row_block, 0)
        return lax.dynamic_update_slice_in_dim(current, swiglu_rows(rows_in, weights), row_start, 0)

    return lax.fori_loop(jnp.zeros((), jnp.int32), block_total, block_step, results)


def route_and_run(tokens, flat_ids, slot_rank, routed, capacity, device_count, own_weights):
    local_tokens, model_width = tokens.shape
    slot_total = flat_ids.shape[0]
    top_count = slot_total // local_tokens
    buffer_rows = device_count * capacity
    padded_rows = (buffer_rows + row_block - 1) // row_block * row_block
    send_slot = jnp.where(routed, flat_ids * capacity + slot_rank, buffer_rows)
    token_of_slot = jnp.arange(slot_total, dtype=jnp.int32) // top_count
    source_row = jnp.zeros((buffer_rows,), jnp.int32).at[send_slot].set(token_of_slot, mode="drop")
    slot_filled = jnp.zeros((buffer_rows,), jnp.int32).at[send_slot].set(1, mode="drop")
    send_counts = jnp.sum(slot_filled.reshape(device_count, capacity), axis=1)
    outgoing = jnp.where(slot_filled[:, None] > 0, tokens[source_row], jnp.zeros((), jnp.bfloat16))
    outgoing = outgoing.reshape(device_count, capacity, model_width)
    count_column = send_counts.astype(jnp.bfloat16).reshape(device_count, 1)
    incoming, arrived = (
        lax.all_to_all(outgoing, "expert", split_axis=0, concat_axis=0, tiled=True),
        lax.all_to_all(count_column, "expert", split_axis=0, concat_axis=0, tiled=True),
    )
    arrived_counts = arrived.reshape(-1).astype(jnp.int32)
    offsets = jnp.cumsum(arrived_counts) - arrived_counts
    live_total = jnp.sum(arrived_counts)
    slot_index = jnp.arange(buffer_rows, dtype=jnp.int32)
    source_of = slot_index // capacity
    within = slot_index % capacity
    is_live = within < arrived_counts[source_of]
    packed_pos = offsets[source_of] + within
    target_pos = jnp.where(is_live, packed_pos, padded_rows)
    compact_source = (
        jnp.full((padded_rows,), buffer_rows, jnp.int32).at[target_pos].set(slot_index, mode="drop")
    )
    flat_incoming = jnp.concatenate(
        [incoming.reshape(buffer_rows, model_width), jnp.zeros((1, model_width), jnp.bfloat16)],
        axis=0,
    )
    compact = flat_incoming[compact_source]
    block_need = (live_total + row_block - 1) // row_block
    results = run_blocks(
        compact, block_need, own_weights, jnp.zeros((padded_rows, model_width), jnp.bfloat16)
    )
    back_slots = results[jnp.where(is_live, packed_pos, 0)]
    back_slots = jnp.where(is_live[:, None], back_slots, jnp.zeros((), jnp.bfloat16))
    back_slots = back_slots.reshape(device_count, capacity, model_width)
    returned_rows = lax.all_to_all(back_slots, "expert", split_axis=0, concat_axis=0, tiled=True)
    picked = returned_rows.reshape(buffer_rows, model_width)[jnp.where(routed, send_slot, 0)]
    return jnp.where(routed[:, None], picked, jnp.zeros((), jnp.bfloat16))


def shards(tokens, expert_ids, gate_weights, w_gate, w_up, w_down):
    device_count = lax.axis_size("expert")
    local_tokens, model_width = tokens.shape
    top_count = expert_ids.shape[1]
    expert_total = device_count * w_gate.shape[0]
    capacity = min(
        local_tokens, 4 * ((local_tokens * top_count + expert_total - 1) // expert_total)
    )
    flat_ids = expert_ids.reshape(-1)
    slot_total = flat_ids.shape[0]
    expert_range = jnp.arange(device_count, dtype=jnp.int32)
    onehot = (flat_ids[:, None] == expert_range[None, :]).astype(jnp.int32)
    slot_rank = jnp.sum(jnp.cumsum(onehot, axis=0) * onehot, axis=1) - 1
    own_weights = (w_gate[0], w_up[0], w_down[0])
    routed = jnp.ones((slot_total,), jnp.bool_)
    slot_values = route_and_run(
        tokens, flat_ids, slot_rank, routed, capacity, device_count, own_weights
    )
    picked = slot_values.reshape(local_tokens, top_count, model_width)
    mixed = jnp.sum(picked.astype(jnp.float32) * gate_weights[:, :, None], axis=1)
    return mixed.astype(jnp.bfloat16)


def solution(mesh):
    placed = (
        P(("groups", "expert"), None),
        P(("groups", "expert"), None),
        P(("groups", "expert"), None),
        P("expert", None, None),
        P("expert", None, None),
        P("expert", None, None),
    )
    return jax.shard_map(
        shards, mesh=mesh, in_specs=placed, out_specs=P(("groups", "expert"), None), check_vma=False
    )
```

profile of v0, /device:TPU:13, one launch (start us, length us, event | category | flops | bytes accessed | tf_op | source)
XLA Modules:
  0.0 305.7 jit_solution(18314291863465316378)
XLA Ops:
  0.0 0.0 copy-start
  0.0 0.8 copy.30
  0.8 0.1 eq.31
  0.9 0.1 eq.27
  1.0 0.7 broadcast_multiply_fusion
  1.7 1.1 reduce-window.19
  2.8 0.2 slice_reduce_fusion
  3.1 0.1 fusion.14
  3.2 0.1 copy.29
  3.3 0.1 mul.40
  3.4 2.4 scatter_custom_fusion
  5.9 0.1 reshape.244
  5.9 0.1 reduce_sum.37
  6.1 0.7 copy.33
  6.8 6.5 %all-to-all-start = ((bf16[16,1,1]{2,1,0:T(2,128)(2,1)}), bf16[16,1,1]{2,1,0:T(2,128)(2,1)S(1)}, u32[]{:S(2)}, u32[]{:S(2)}) async-start(bf16[16,1,1]{2,1,0:T(2,128)(2,1)} %copy.33), calls=%async_computation | async-start | bytes 16384 | tf_op jit(solution)/shard_map/all_to_all | solution.py:42
  13.3 0.1 broadcast_in_dim.61
  13.4 2.4 scatter_custom_fusion.1
  15.9 6.0 %gather_fusion = bf16[1024,2048]{1,0:T(8,128)(2,1)} fusion(bf16[64,2048]{1,0:T(8,128)(2,1)S(1)} %copy-done, s32[1024]{0:T(1024)S(1)} %fusion.20), kind=kCustom, calls=%fused_computation | custom fusion | bytes 8392704 | tf_op jit(solution)/shard_map/gather | solution.py:37
  21.9 4.5 %broadcast_select_fusion = bf16[16,64,2048]{2,1,0:T(8,128)(2,1)} fusion(bf16[16,64,2048]{2,1,0:T(8,128)(2,1)} %bitcast.78, pred[16,64]{1,0:T(8,128)(4,1)S(1)} %broadcast_in_dim.61), kind=kLoop, calls=%fused_computation.20 | loop fusion | flops 2097152 | bytes 8389632 | tf_op jit(solution)/shard_map/jit(_where)/select_n | solution.py:37
  26.4 0.0 all-to-all-done
  26.4 6.0 %all-to-all-start.1 = ((bf16[16,64,2048]{2,1,0:T(8,128)(2,1)}), bf16[16,64,2048]{2,1,0:T(8,128)(2,1)}, u32[]{:S(2)}, u32[]{:S(2)}) async-start(bf16[16,64,2048]{2,1,0:T(8,128)(2,1)} %broadcast_select_fusion), calls=%async_computation.1 | async-start | bytes 8388608 | tf_op jit(solution)/shard_map/all_to_all | solution.py:41
  32.7 0.9 convert_reduce_fusion.1
  34.3 0.1 reduce.11
  34.4 0.6 fusion.33
  35.1 4.2 %compare_select_fusion.6 = s32[1024,1]{0,1:T(1,128)S(1)} fusion(s32[]{:T(128)} %bitcast.13, s32[]{:T(128)} %bitcast.14, s32[]{:T(128)} %bitcast.15, s32[]{:T(128)} %bitcast.16, s32[]{:T(128)} %bitcast.17, s32[]{:T(128)} %bitcast.19, s32[]{:T(128)} %bitcast.18), kind=kLoop, calls=%fused_computation.48 | loop fusion | flops 23552 | bytes 4124 | tf_op jit(solution)/shard_map/gather | solution.py:50
  39.3 5.7 %select_select_fusion.1 = s32[1024]{0:T(1024)S(1)} fusion(pred[1024]{0:T(1024)(128)(4,1)S(1)} %compare_reduce_fusion, pred[1024]{0:T(1024)(128)(4,1)S(1)} %compare_reduce_fusion.1, pred[1024]{0:T(1024)(128)(4,1)S(1)} %compare_reduce_fusion.2, pred[1024]{0:T(1024)(128)(4,1)S(1)} %compare_reduce_fusion.3, pred[1024]{0:T(1024)(128)(4,1)S(1)} %compare_reduce_fusion.4, ...), kind=kLoop, calls=%fused_computation.72 | loop fusion | flops 9216 | bytes 17444 | tf_op jit(solution)/shard_map/gather | solution.py:50
  45.0 0.1 gather.29
  45.1 0.7 fusion.34
  45.8 4.5 %compare_select_fusion.7 = s32[1024,1]{0,1:T(1,128)S(1)} fusion(s32[]{:T(128)} %bitcast.34, s32[]{:T(128)} %bitcast.35, s32[]{:T(128)} %bitcast.36, s32[]{:T(128)} %bitcast.37, s32[]{:T(128)} %bitcast.38, s32[]{:T(128)} %bitcast.40, s32[]{:T(128)} %bitcast.39), kind=kLoop, calls=%fused_computation.49 | loop fusion | flops 23552 | bytes 4124 | tf_op jit(solution)/shard_map/gather | solution.py:51
  50.3 5.4 %select_select_fusion = s32[1024]{0:T(1024)S(1)} fusion(pred[1024]{0:T(1024)(128)(4,1)S(1)} %compare_reduce_fusion, pred[1024]{0:T(1024)(128)(4,1)S(1)} %compare_reduce_fusion.1, pred[1024]{0:T(1024)(128)(4,1)S(1)} %compare_reduce_fusion.2, pred[1024]{0:T(1024)(128)(4,1)S(1)} %compare_reduce_fusion.3, pred[1024]{0:T(1024)(128)(4,1)S(1)} %compare_reduce_fusion.4, ...), kind=kLoop, calls=%fused_computation.71 | loop fusion | flops 9216 | bytes 17444 | tf_op jit(solution)/shard_map/gather | solution.py:51
  55.8 4.3 %scatter_custom_fusion.2 = s32[1024]{0:T(1024)S(1)} fusion(s32[1024]{0:T(1024)S(1)} %bitcast.89, s32[1024]{0:T(1024)S(1)} %iota.46, s32[]{:T(128)} %constant.94.clone.1), kind=kCustom, calls=%fused_computation.80 | custom fusion | bytes 4100 | tf_op jit(solution)/shard_map/scatter | solution.py:54
  60.2 64.7 %all-to-all-done.1 = bf16[16,64,2048]{2,1,0:T(8,128)(2,1)} async-done(((bf16[16,64,2048]{2,1,0:T(8,128)(2,1)}), bf16[16,64,2048]{2,1,0:T(8,128)(2,1)}, u32[]{:S(2)}, u32[]{:S(2)}) %all-to-all-start.1) | async-done | bytes 4194336 | tf_op jit(solution)/shard_map/all_to_all | solution.py:41
  124.8 4.7 %concatenate.3 = bf16[1025,2048]{1,0:T(8,128)(2,1)} pad(bf16[1024,2048]{1,0:T(8,128)(2,1)} %bitcast.22, bf16[]{:T(256)} %constant.98.clone.1), padding=0_1x0_0 | pad | bytes 8392706 | tf_op jit(solution)/shard_map/concatenate | solution.py:56
  129.6 11.6 %gather_fusion.1 = bf16[1024,2048]{1,0:T(8,128)(2,1)} fusion(bf16[1025,2048]{1,0:T(8,128)(2,1)} %concatenate.3, s32[1024]{0:T(1024)S(1)} %fusion.21), kind=kCustom, calls=%fused_computation.1 | custom fusion | bytes 8392704 | tf_op jit(solution)/shard_map/gather | solution.py:60
  141.1 2.5 broadcast_in_dim.60
  143.6 0.4 copy-done.2
  144.0 19.3 %while.10 = (s32[]{:T(128)}, bf16[1024,2048]{1,0:T(8,128)(2,1)}, s32[]{:T(128)}, bf16[1024,2048]{1,0:T(8,128)(2,1)}, bf16[2048,768]{1,0:T(8,128)(2,1)S(1)}, /*in...) while((s32[]{:T(128)}, bf16[1024,2048]{1,0:T(8,128)(2,1)}, ...), condition=%wide.region_10.11_spmd, body=%wide.region_9.10_spmd.sunk | while | flops 2417623040 | bytes 14156959 | solution.py:23
  144.0 3.1 %fusion.50 = f32[256,768]{1,0:T(8,128)} fusion(bf16[2048,768]{1,0:T(8,128)(2,1)S(1)} %get-tuple-element.164, bf16[1024,2048]{1,0:T(8,128)(2,1)} %get-tuple-element.163, s32[]{:T(128)S(6)} %select_n.234), kind=kOutput, calls=%fused_computation.12.clone.1 | convolution fusion | flops 805306368 | bytes 4980740 | tf_op jit(solution)/shard_map/while/body/dot_general | solution.py:10
  147.2 6.6 %fusion.51 = bf16[1024,2048]{1,0:T(8,128)(2,1)} fusion(bf16[1024,2048]{1,0:T(8,128)(2,1)} %get-tuple-element.150, s32[]{:T(128)S(6)} %select_n.234, bf16[768,2048]{1,0:T(8,128)(2,1)} %get-tuple-element.166, bf16[2048,768]{1,0:T(8,128)(2,1)} %get-tuple-element.165, bf16[1024,2048]{1,0:T(8,128)(2,1)} %get-tuple-element.163, f32[256,768]{1,0:T(8,128)} %fusion.50), kind=kOutput, calls=%fused_computation.8.clone.1 | convolution fusion | flops 1612316672 | bytes 9176064 | tf_op jit(solution)/shard_map/while/body/dot_general | solution.py:13
  153.7 3.1 %fusion.50 = f32[256,768]{1,0:T(8,128)} fusion(bf16[2048,768]{1,0:T(8,128)(2,1)S(1)} %get-tuple-element.164, bf16[1024,2048]{1,0:T(8,128)(2,1)} %get-tuple-element.163, s32[]{:T(128)S(6)} %select_n.234), kind=kOutput, calls=%fused_computation.12.clone.1 | convolution fusion | flops 805306368 | bytes 4980740 | tf_op jit(solution)/shard_map/while/body/dot_general | solution.py:10
  156.9 6.5 %fusion.51 = bf16[1024,2048]{1,0:T(8,128)(2,1)} fusion(bf16[1024,2048]{1,0:T(8,128)(2,1)} %get-tuple-element.150, s32[]{:T(128)S(6)} %select_n.234, bf16[768,2048]{1,0:T(8,128)(2,1)} %get-tuple-element.166, bf16[2048,768]{1,0:T(8,128)(2,1)} %get-tuple-element.165, bf16[1024,2048]{1,0:T(8,128)(2,1)} %get-tuple-element.163, f32[256,768]{1,0:T(8,128)} %fusion.50), kind=kOutput, calls=%fused_computation.8.clone.1 | convolution fusion | flops 1612316672 | bytes 9176064 | tf_op jit(solution)/shard_map/while/body/dot_general | solution.py:13
  163.3 11.6 %gather_fusion.2 = bf16[1024,2048]{1,0:T(8,128)(2,1)} fusion(bf16[1024,2048]{1,0:T(8,128)(2,1)} %get-tuple-element.43, s32[1024]{0:T(1024)S(1)} %broadcast_clamp_fusion), kind=kCustom, calls=%fused_computation.2 | custom fusion | bytes 8392704 | tf_op jit(solution)/shard_map/gather | solution.py:65
  174.9 4.5 %broadcast_select_fusion.1 = bf16[16,64,2048]{2,1,0:T(8,128)(2,1)} fusion(bf16[16,64,2048]{2,1,0:T(8,128)(2,1)} %bitcast.77, pred[16,64]{1,0:T(8,128)(4,1)S(1)} %fusion.16), kind=kLoop, calls=%fused_computation.21 | loop fusion | flops 2097152 | bytes 8389632 | tf_op jit(solution)/shard_map/jit(_where)/select_n | solution.py:66
  179.4 24.2 %all-to-all-start.2 = ((bf16[16,64,2048]{2,1,0:T(8,128)(2,1)}), bf16[16,64,2048]{2,1,0:T(8,128)(2,1)}, u32[]{:S(2)}, u32[]{:S(2)}) async-start(bf16[16,64,2048]{2,1,0:T(8,128)(2,1)} %broadcast_select_fusion.1), calls=%async_computation.2 | async-start | bytes 8388608 | tf_op jit(solution)/shard_map/all_to_all | solution.py:68
  203.6 0.1 copy.35
  203.7 92.4 %all-to-all-done.2 = bf16[16,64,2048]{2,1,0:T(8,128)(2,1)} async-done(((bf16[16,64,2048]{2,1,0:T(8,128)(2,1)}), bf16[16,64,2048]{2,1,0:T(8,128)(2,1)}, u32[]{:S(2)}, u32[]{:S(2)}) %all-to-all-start.2) | async-done | bytes 4194336 | tf_op jit(solution)/shard_map/all_to_all | solution.py:68
  296.0 7.1 %gather_fusion.3 = bf16[512,2048]{1,0:T(8,128)(2,1)S(1)} fusion(bf16[1024,2048]{1,0:T(8,128)(2,1)} %bitcast.49, s32[1024]{0:T(1024)S(1)} %pad_clamp_fusion), kind=kCustom, calls=%fused_computation.3 | custom fusion | bytes 4196352 | tf_op jit(solution)/shard_map/gather | solution.py:69
  303.2 2.5 fusion.12
  (32 shorter events, 0.5 us)
Async XLA Ops:
  0.0 15.9 %copy-start = (bf16[64,2048]{1,0:T(8,128)(2,1)S(1)}, bf16[64,2048]{1,0:T(8,128)(2,1)}, u32[]{:S(2)}) copy-start(bf16[64,2048]{1,0:T(8,128)(2,1)} %param.8) | copy-start | bytes 786436
  6.8 19.6 %all-to-all-start = ((bf16[16,1,1]{2,1,0:T(2,128)(2,1)}), bf16[16,1,1]{2,1,0:T(2,128)(2,1)S(1)}, u32[]{:S(2)}, u32[]{:S(2)}) async-start(bf16[16,1,1]{2,1,0:T(2,128)(2,1)} %copy.33), calls=%async_computation | async-start | bytes 16384 | tf_op jit(solution)/shard_map/all_to_all | solution.py:42
  26.4 98.5 %all-to-all-start.1 = ((bf16[16,64,2048]{2,1,0:T(8,128)(2,1)}), bf16[16,64,2048]{2,1,0:T(8,128)(2,1)}, u32[]{:S(2)}, u32[]{:S(2)}) async-start(bf16[16,64,2048]{2,1,0:T(8,128)(2,1)} %broadcast_select_fusion), calls=%async_computation.1 | async-start | bytes 8388608 | tf_op jit(solution)/shard_map/all_to_all | solution.py:41
  141.1 2.9 copy-start.2
  179.4 24.2 %copy-start.1 = (f32[64,8]{0,1:T(8,128)S(1)}, f32[64,8]{0,1:T(8,128)}, u32[]{:S(2)}) copy-start(f32[64,8]{0,1:T(8,128)} %param.10) | copy-start | bytes 6148
  179.4 116.6 %all-to-all-start.2 = ((bf16[16,64,2048]{2,1,0:T(8,128)(2,1)}), bf16[16,64,2048]{2,1,0:T(8,128)(2,1)}, u32[]{:S(2)}, u32[]{:S(2)}) async-start(bf16[16,64,2048]{2,1,0:T(8,128)(2,1)} %broadcast_select_fusion.1), calls=%async_computation.2 | async-start | bytes 8388608 | tf_op jit(solution)/shard_map/all_to_all | solution.py:68
where the time goes:
time: 307 us; the launch traced here: 306 us
  waiting for transfers between devices  157 us (51%)
  local copies, waits for them, and re-layouts  56.8 us (19%)
  starting transfers between devices  36.7 us (12%)
  other arithmetic  35 us (11%)
  matrix products  19.3 us (6%)
    all_to_all x1, waiting for transfers between devices, route_and_run(): lax.all_to_all(back_slots, 'expert', split_axis=0, concat_axis=0, tiled=T...  92.4 us
    all_to_all x1, waiting for transfers between devices, route_and_run(): lax.all_to_all(outgoing, 'expert', split_axis=0, concat_axis=0, tiled=True)  64.7 us
    all_to_all x1, starting transfers between devices, route_and_run(): lax.all_to_all(back_slots, 'expert', split_axis=0, concat_axis=0, tiled=T...  24.2 us
    dot_general x2, matrix products, swiglu_rows(): jnp.dot(hidden, weights[2], preferred_element_type=jnp.float32)  13.1 us
    gather x1, local copies, waits for them, and re-layouts, route_and_run(): compact = flat_incoming[compact_source]  11.6 us
    gather x1, local copies, waits for them, and re-layouts, route_and_run(): back_slots = results[jnp.where(is_live, packed_pos, 0)]  11.6 us
    gather x11, other arithmetic, route_and_run(): is_live = within < arrived_counts[source_of]  10.2 us
    gather x2, other arithmetic, route_and_run(): packed_pos = offsets[source_of] + within  9.94 us
  transfers between devices with their start and end apart: 3, of which 2 were waited for; matrix products, arithmetic and copies ran while one was open for 13% of the time, Pallas kernels for 0%

commit v1 on v0

--- a/solution.py
+++ b/solution.py
@@ -1,9 +1,16 @@
+import functools
 import jax
 import jax.numpy as jnp
 from jax import lax
+from jax.experimental import pallas as pl
+from jax.experimental.pallas import tpu as pltpu
 from jax.sharding import PartitionSpec as P
 
 row_block = 256
+pieces = 2
+hidden_tile = 256
+out_tile = 512
+vmem_budget = 48 * 2**20
 
 
 def swiglu_rows(rows_in, weights):
@@ -70,6 +77,289 @@
     return jnp.where(routed[:, None], picked, jnp.zeros((), jnp.bfloat16))
 
 
+def visit_order(depth, place):
+    return sorted(range(depth), key=lambda g: (abs(g - place), g if 2 * place < depth else -g))
+
+
+def fused_kernel(
+    depth, x_hbm, t_hbm, wg_hbm, wu_hbm, wd_hbm, out_ref,
+    rows, tiles, wg, wu, wd, hid, part, a_in, y_out, y_in, c_out, c_in, acc,
+    w_sem, own_sem, sx, rx, st, rt, sa, ra, sy, ry, sc, rc,
+):
+    f32, bf16 = jnp.float32, jnp.bfloat16
+    local, width = x_hbm.shape
+    inner = wg.shape[1]
+    me = lax.axis_index("expert")
+    c = lax.rem(me, 2)
+    y = lax.rem(me // 2, 2)
+    z = me // 4
+    own_slot = y * 2 + c
+    group_of = []
+    for step in range(depth):
+        g = jnp.int32(0)
+        for place in range(depth):
+            g = g + jnp.where(z == place, visit_order(depth, place)[step], 0)
+        group_of.append(g)
+    sibling = {"expert": (z * 2 + y) * 2 + (1 - c)}
+    across = {"expert": (z * 2 + (1 - y)) * 2 + c}
+
+    def along(place):
+        return {"expert": (place * 2 + y) * 2 + c}
+
+    has_up, has_down = z < depth - 1, z > 0
+
+    def signal(target):
+        pl.semaphore_signal(barrier, inc=1, device_id=target, device_id_type=pl.DeviceIdType.MESH)
+
+    barrier = pltpu.get_barrier_semaphore()
+    signal(sibling)
+    signal(across)
+    pl.when(has_up)(lambda: signal(along(z + 1)))
+    pl.when(has_down)(lambda: signal(along(z - 1)))
+    pl.semaphore_wait(barrier, 2 + has_up.astype(jnp.int32) + has_down.astype(jnp.int32))
+
+    def remote(src, dst, send, recv, target):
+        return pltpu.make_async_remote_copy(
+            src_ref=src, dst_ref=dst, send_sem=send, recv_sem=recv,
+            device_id=target, device_id_type=pl.DeviceIdType.MESH,
+        )
+
+    pending = []
+
+    def launch(copies, cond=None):
+        def go():
+            for copy in copies:
+                copy.start()
+        if cond is None:
+            go()
+        else:
+            pl.when(cond)(go)
+        pending.append((copies, cond))
+
+    def block_copies(g, slot, src_x, src_t, at, target):
+        return [
+            remote(src_t, tiles.at[g, slot], st.at[at], rt.at[g, slot], target),
+            remote(src_x, rows.at[g, slot], sx.at[at], rx.at[g, slot], target),
+        ]
+
+    def push(g, slot, at, target, cond=None):
+        launch(block_copies(g, slot, rows.at[g, slot], tiles.at[g, slot], at, target), cond)
+
+    def arrive(g, slot):
+        for copy in block_copies(g, slot, rows.at[g, slot], tiles.at[g, slot], 0, sibling):
+            copy.wait_recv()
+
+    y_base, c_base = depth + 1, 2 * depth + 1
+    launch(block_copies(z, own_slot, x_hbm, t_hbm, 0, along(z + 1)), has_up)
+    launch(block_copies(z, own_slot, x_hbm, t_hbm, 1, along(z - 1)), has_down)
+    launch(block_copies(z, own_slot, x_hbm, t_hbm, y_base, across))
+    launch(block_copies(z, own_slot, x_hbm, t_hbm, c_base, sibling))
+    own_copies = [
+        pltpu.make_async_copy(x_hbm, rows.at[z, own_slot], own_sem.at[0]),
+        pltpu.make_async_copy(t_hbm, tiles.at[z, own_slot], own_sem.at[1]),
+    ]
+    weight_copies = [
+        pltpu.make_async_copy(wg_hbm.at[0], wg, w_sem.at[0]),
+        pltpu.make_async_copy(wu_hbm.at[0], wu, w_sem.at[1]),
+        pltpu.make_async_copy(wd_hbm.at[0], wd, w_sem.at[2]),
+    ]
+    for copy in own_copies + weight_copies:
+        copy.start()
+
+    def relay_chain(step):
+        g = group_of[step]
+        arrive(g, own_slot)
+        onward = jnp.where(g < z, z + 1, z - 1)
+        push(g, own_slot, 1 + step, along(onward), (onward >= 0) & (onward < depth))
+        push(g, own_slot, y_base + step, across)
+        push(g, own_slot, c_base + step, sibling)
+
+    def relay_across(step):
+        g = group_of[step]
+        slot = (1 - y) * 2 + c
+        arrive(g, slot)
+        push(g, slot, c_base + depth + step, sibling)
+        arrive(g, y * 2 + 1 - c)
+        arrive(g, (1 - y) * 2 + 1 - c)
+
+    def piece_of(p):
+        return pl.ds(p * (width // pieces), width // pieces)
+
+    def pair_copy(step, half, p):
+        g = group_of[step]
+        return remote(
+            part.at[g, half * 2 + 1 - c, :, piece_of(p)], a_in.at[g, half, :, piece_of(p)],
+            sa.at[step, half, p], ra.at[step, half, p], sibling,
+        )
+
+    def run_group(step):
+        g = group_of[step]
+
+        def hidden_step(j, carry):
+            cols = pl.ds(pl.multiple_of(j * hidden_tile, hidden_tile), hidden_tile)
+            block = rows[g].reshape(4 * local, width)
+            gate = jnp.dot(block, wg[:, cols], preferred_element_type=f32)
+            up = jnp.dot(block, wu[:, cols], preferred_element_type=f32)
+            hid[:, cols] = (gate / (1.0 + jnp.exp(-gate)) * up).astype(bf16)
+            return carry
+
+        lax.fori_loop(0, inner // hidden_tile, hidden_step, 0)
+        span = tiles.shape[3]
+        lane = lax.broadcasted_iota(jnp.int32, (local, span), 1)
+        line = lax.broadcasted_iota(jnp.int32, (local, span), 0)
+        diagonal = (lane == line) | (lane == line + local)
+        expert_row = lax.broadcasted_iota(jnp.int32, tiles.shape[2:], 0) == me
+        scales = []
+        for slot in range(4):
+            mine = jnp.sum(
+                jnp.where(expert_row, tiles[g, slot].astype(f32), 0.0), axis=0, keepdims=True
+            )
+            spread = jnp.broadcast_to(mine, (local, span))
+            scales.append(jnp.sum(jnp.where(diagonal, spread, 0.0), axis=1, keepdims=True))
+        for p in range(pieces):
+
+            def out_step(j, carry):
+                first = pl.multiple_of(p * (width // pieces) + j * out_tile, out_tile)
+                cols = pl.ds(first, out_tile)
+                result = jnp.dot(hid[...], wd[:, cols], preferred_element_type=f32)
+                for slot in range(4):
+                    scaled = result[slot * local : (slot + 1) * local] * scales[slot]
+                    part[g, slot, :, cols] = scaled.astype(bf16)
+                return carry
+
+            lax.fori_loop(0, width // pieces // out_tile, out_step, 0)
+            for half in range(2):
+                launch([pair_copy(step, half, p)])
+
+    def pair_sum(g, half, cols):
+        return part[g, half * 2 + c, :, cols].astype(f32) + a_in[g, half, :, cols].astype(f32)
+
+    def across_copy(step, p):
+        return remote(
+            y_out.at[step, :, piece_of(p)], y_in.at[step, :, piece_of(p)],
+            sy.at[step, p], ry.at[step, p], across,
+        )
+
+    def send_across(step):
+        g = group_of[step]
+        for p in range(pieces):
+            for half in range(2):
+                pair_copy(step, half, p).wait_recv()
+            y_out[step, :, piece_of(p)] = pair_sum(g, 1 - y, piece_of(p)).astype(bf16)
+            launch([across_copy(step, p)])
+
+    def chain_copy(step, way, g, p, target):
+        return remote(
+            c_out.at[step, :, piece_of(p)], c_in.at[way, g, :, piece_of(p)],
+            sc.at[step, p], rc.at[way, g, p], target,
+        )
+
+    def add_chain(way, g, p):
+        chain_copy(0, way, g, p, sibling).wait_recv()
+        acc[...] += c_in[way, g, :, piece_of(p)].astype(f32)
+
+    def send_chain(step):
+        g = group_of[step]
+        for p in range(pieces):
+            cols = piece_of(p)
+            across_copy(step, p).wait_recv()
+            acc[...] = pair_sum(g, y, cols) + y_in[step, :, cols].astype(f32)
+            if step == 0:
+                pl.when(has_down)(lambda: add_chain(0, g, p))
+                pl.when(has_up)(lambda: add_chain(1, g, p))
+                out_ref[:, cols] = acc[...].astype(bf16)
+            else:
+                way = jnp.where(g > z, 0, 1)
+                pl.when(((g > z) & has_down) | ((g < z) & has_up))(lambda: add_chain(way, g, p))
+                c_out[step, :, cols] = acc[...].astype(bf16)
+                launch([chain_copy(step, way, g, p, along(jnp.where(g > z, z + 1, z - 1)))])
+
+    for copy in own_copies:
+        copy.wait()
+    for step in range(depth):
+        if step + 1 < depth:
+            relay_chain(step + 1)
+        relay_across(step)
+        if step == 0:
+            for copy in weight_copies:
+                copy.wait()
+        if step == depth - 1 and depth > 2:
+            send_across(step - 1)
+        run_group(step)
+    order = [depth - 2, depth - 1] + list(range(depth - 3, -1, -1))
+    for step in order[1 if depth > 2 else 0 :]:
+        send_across(step)
+    for step in order:
+        send_chain(step)
+    for copies, cond in pending:
+        def finish(copies=copies):
+            for copy in copies:
+                copy.wait_send()
+        if cond is None:
+            finish()
+        else:
+            pl.when(cond)(finish)
+
+
+def fused_layer(tokens, tile, w_gate, w_up, w_down, depth):
+    local, width = tokens.shape
+    inner = w_gate.shape[2]
+    bf16, f32 = jnp.bfloat16, jnp.float32
+    dma = pltpu.SemaphoreType.DMA
+    anywhere = pl.BlockSpec(memory_space=pl.ANY)
+    sends = 4 * depth + 1
+    return pl.pallas_call(
+        functools.partial(fused_kernel, depth),
+        out_shape=jax.ShapeDtypeStruct((local, width), bf16),
+        in_specs=[anywhere] * 5,
+        out_specs=pl.BlockSpec(memory_space=pltpu.VMEM),
+        scratch_shapes=[
+            pltpu.VMEM((depth, 4, local, width), bf16),
+            pltpu.VMEM((depth, 4) + tile.shape, bf16),
+            pltpu.VMEM((width, inner), bf16),
+            pltpu.VMEM((width, inner), bf16),
+            pltpu.VMEM((inner, width), bf16),
+            pltpu.VMEM((4 * local, inner), bf16),
+            pltpu.VMEM((depth, 4, local, width), bf16),
+            pltpu.VMEM((depth, 2, local, width), bf16),
+            pltpu.VMEM((depth, local, width), bf16),
+            pltpu.VMEM((depth, local, width), bf16),
+            pltpu.VMEM((depth, local, width), bf16),
+            pltpu.VMEM((2, depth, local, width), bf16),
+            pltpu.VMEM((local, width // pieces), f32),
+            dma((3,)), dma((2,)),
+            dma((sends,)), dma((depth, 4)), dma((sends,)), dma((depth, 4)),
+            dma((depth, 2, pieces)), dma((depth, 2, pieces)),
+            dma((depth, pieces)), dma((depth, pieces)),
+            dma((depth, pieces)), dma((2, depth, pieces)),
+        ],
+        compiler_params=pltpu.CompilerParams(
+            collective_id=0, has_side_effects=True, vmem_limit_bytes=60 * 2**20
+        ),
+    )(tokens, tile, w_gate, w_up, w_down)
+
+
+def choice_tile(expert_ids, gate_weights, expert_total):
+    experts = jnp.arange(expert_total, dtype=jnp.int32)[:, None, None]
+    chosen = experts == expert_ids[None, :, :]
+    dense = jnp.sum(jnp.where(chosen, gate_weights[None, :, :], 0.0), axis=2)
+    high = lax.reduce_precision(dense, 8, 7)
+    return jnp.concatenate([high, dense - high], axis=1).astype(jnp.bfloat16)
+
+
+def fits_fused(device_count, local_tokens, model_width, inner):
+    gathered = 2 * device_count * local_tokens * model_width
+    weights = 6 * model_width * inner
+    return (
+        device_count % 4 == 0
+        and device_count >= 8
+        and 2 * local_tokens % 128 == 0
+        and model_width % (pieces * out_tile) == 0
+        and inner % hidden_tile == 0
+        and 4 * gathered + weights <= vmem_budget
+    )
+
+
 def shards(tokens, expert_ids, gate_weights, w_gate, w_up, w_down):
     device_count = lax.axis_size("expert")
     local_tokens, model_width = tokens.shape
@@ -78,6 +368,9 @@
     capacity = min(
         local_tokens, 4 * ((local_tokens * top_count + expert_total - 1) // expert_total)
     )
+    if fits_fused(device_count, local_tokens, model_width, w_gate.shape[2]):
+        tile = choice_tile(expert_ids, gate_weights, expert_total)
+        return fused_layer(tokens, tile, w_gate, w_up, w_down, device_count // 4)
     flat_ids = expert_ids.reshape(-1)
     slot_total = flat_ids.shape[0]
     expert_range = jnp.arange(device_count, dtype=jnp.int32)

time: 307 us -> 72.7 us (0.24)
  the two profiles are of different devices: /device:TPU:13 before, /device:TPU:0 now
where the time goes in v1:
time: 72.7 us; the launch traced here: 72.5 us
  Pallas kernels  69.4 us (95%)
  local copies, waits for them, and re-layouts  1.67 us (2%)
  other arithmetic  1.4 us (2%)
    pallas_call x1, Pallas kernels, fused_layer(): pl.pallas_call(functools.partial(fused_kernel, depth), out_shape=jax.Shap...  69.4 us
    unnamed x1, local copies, waits for them, and re-layouts  1.67 us

profile of v1, /device:TPU:0, one launch (start us, length us, event | category | flops | bytes accessed | tf_op | source)
XLA Modules:
  0.0 72.5 jit_solution(12072396318060270739)
XLA Ops:
  0.0 0.7 %select_reduce_fusion = f32[16,64]{1,0:T(8,128)S(1)} fusion(f32[64,8]{0,1:T(8,128)} %param.8, s32[64,8]{0,1:T(8,128)} %param.7), kind=kLoop, calls=%fused_computation | loop fusion | flops 23552 | bytes 8192 | tf_op jit(solution)/shard_map/reduce_sum | solution.py:345
  0.7 0.7 pad_maximum_fusion.t_hbm
  1.4 69.4 %shard_map.64 = bf16[64,2048]{1,0:T(8,128)(2,1)} custom-call(bf16[64,2048]{1,0:T(8,128)(2,1)} %x_hbm.1, bf16[16,128]{1,0:T(8,128)(2,1)} %pad_maximum_fusion.t_hbm, bf16[1,2048,768]{2,1,0:T(8,128)(2,1)} %wg_hbm.1, bf16[1,2048,768]{2,1,0:T(8,128)(2,1)} %wu_hbm.1, bf16[1,768,2048]{2,1,0:T(8,128)(2,1)} %wd_hbm.1), custom_call_target="tpu_custom_call" | custom-call | tf_op jit(solution)/shard_map/pallas_call | solution.py:311
  70.8 1.7 %copy.10 = bf16[64,2048]{1,0:T(8,128)(2,1)} copy(bf16[64,2048]{1,0:T(8,128)(2,1)} %shard_map.64) | data formatting | bytes 524288
  (1 shorter events, 0.0 us)

commit v2 on v1

--- a/solution.py
+++ b/solution.py
@@ -7,9 +7,9 @@
 from jax.sharding import PartitionSpec as P
 
 row_block = 256
-pieces = 2
+pieces = 4
+chunks = 4
 hidden_tile = 256
-out_tile = 512
 vmem_budget = 48 * 2**20
 
 
@@ -136,24 +136,34 @@
             pl.when(cond)(go)
         pending.append((copies, cond))
 
-    def block_copies(g, slot, src_x, src_t, at, target):
-        return [
-            remote(src_t, tiles.at[g, slot], st.at[at], rt.at[g, slot], target),
-            remote(src_x, rows.at[g, slot], sx.at[at], rx.at[g, slot], target),
+    chunk_rows = local // chunks
+
+    def chunk_copies(g, slot, h, src_x, src_t, at, target):
+        part_rows = pl.ds(h * chunk_rows, chunk_rows)
+        copies = [
+            remote(
+                src_x.at[part_rows], rows.at[g, slot, part_rows],
+                sx.at[at, h], rx.at[g, slot, h], target,
+            )
         ]
-
-    def push(g, slot, at, target, cond=None):
-        launch(block_copies(g, slot, rows.at[g, slot], tiles.at[g, slot], at, target), cond)
-
-    def arrive(g, slot):
-        for copy in block_copies(g, slot, rows.at[g, slot], tiles.at[g, slot], 0, sibling):
+        if h == 0:
+            copies.append(remote(src_t, tiles.at[g, slot], st.at[at], rt.at[g, slot], target))
+        return copies
+
+    def push(g, slot, h, at, target, cond=None):
+        launch(chunk_copies(g, slot, h, rows.at[g, slot], tiles.at[g, slot], at, target), cond)
+
+    def arrive(g, slot, h):
+        for copy in chunk_copies(g, slot, h, rows.at[g, slot], tiles.at[g, slot], 0, sibling):
             copy.wait_recv()
 
     y_base, c_base = depth + 1, 2 * depth + 1
-    launch(block_copies(z, own_slot, x_hbm, t_hbm, 0, along(z + 1)), has_up)
-    launch(block_copies(z, own_slot, x_hbm, t_hbm, 1, along(z - 1)), has_down)
-    launch(block_copies(z, own_slot, x_hbm, t_hbm, y_base, across))
-    launch(block_copies(z, own_slot, x_hbm, t_hbm, c_base, sibling))
+    for h in range(chunks):
+        launch(chunk_copies(z, own_slot, h, x_hbm, t_hbm, 0, along(z + 1)), has_up)
+        launch(chunk_copies(z, own_slot, h, x_hbm, t_hbm, 1, along(z - 1)), has_down)
+        launch(chunk_copies(z, own_slot, h, x_hbm, t_hbm, y_base, across))
+    for h in range(chunks):
+        launch(chunk_copies(z, own_slot, h, x_hbm, t_hbm, c_base, sibling))
     own_copies = [
         pltpu.make_async_copy(x_hbm, rows.at[z, own_slot], own_sem.at[0]),
         pltpu.make_async_copy(t_hbm, tiles.at[z, own_slot], own_sem.at[1]),
@@ -166,21 +176,25 @@
     for copy in own_copies + weight_copies:
         copy.start()
 
-    def relay_chain(step):
-        g = group_of[step]
-        arrive(g, own_slot)
+    def relay_chain(step, h):
+        g = group_of[step]
+        arrive(g, own_slot, h)
         onward = jnp.where(g < z, z + 1, z - 1)
-        push(g, own_slot, 1 + step, along(onward), (onward >= 0) & (onward < depth))
-        push(g, own_slot, y_base + step, across)
-        push(g, own_slot, c_base + step, sibling)
-
-    def relay_across(step):
+        push(g, own_slot, h, 1 + step, along(onward), (onward >= 0) & (onward < depth))
+        push(g, own_slot, h, y_base + step, across)
+        push(g, own_slot, h, c_base + step, sibling)
+
+    def relay_across(step, h):
         g = group_of[step]
         slot = (1 - y) * 2 + c
-        arrive(g, slot)
-        push(g, slot, c_base + depth + step, sibling)
-        arrive(g, y * 2 + 1 - c)
-        arrive(g, (1 - y) * 2 + 1 - c)
+        arrive(g, slot, h)
+        push(g, slot, h, c_base + depth + step, sibling)
+
+    def await_sibling(step):
+        g = group_of[step]
+        for h in range(chunks):
+            arrive(g, y * 2 + 1 - c, h)
+            arrive(g, (1 - y) * 2 + 1 - c, h)
 
     def piece_of(p):
         return pl.ds(p * (width // pieces), width // pieces)
@@ -192,18 +206,16 @@
             sa.at[step, half, p], ra.at[step, half, p], sibling,
         )
 
-    def run_group(step):
-        g = group_of[step]
-
-        def hidden_step(j, carry):
-            cols = pl.ds(pl.multiple_of(j * hidden_tile, hidden_tile), hidden_tile)
-            block = rows[g].reshape(4 * local, width)
-            gate = jnp.dot(block, wg[:, cols], preferred_element_type=f32)
-            up = jnp.dot(block, wu[:, cols], preferred_element_type=f32)
-            hid[:, cols] = (gate / (1.0 + jnp.exp(-gate)) * up).astype(bf16)
-            return carry
-
-        lax.fori_loop(0, inner // hidden_tile, hidden_step, 0)
+    def run_hidden(step, j):
+        g = group_of[step]
+        cols = pl.ds(j * hidden_tile, hidden_tile)
+        block = rows[g].reshape(4 * local, width)
+        gate = jnp.dot(block, wg[:, cols], preferred_element_type=f32)
+        up = jnp.dot(block, wu[:, cols], preferred_element_type=f32)
+        hid[:, cols] = (gate / (1.0 + jnp.exp(-gate)) * up).astype(bf16)
+
+    def run_out(step):
+        g = group_of[step]
         span = tiles.shape[3]
         lane = lax.broadcasted_iota(jnp.int32, (local, span), 1)
         line = lax.broadcasted_iota(jnp.int32, (local, span), 0)
@@ -217,19 +229,27 @@
             spread = jnp.broadcast_to(mine, (local, span))
             scales.append(jnp.sum(jnp.where(diagonal, spread, 0.0), axis=1, keepdims=True))
         for p in range(pieces):
-
-            def out_step(j, carry):
-                first = pl.multiple_of(p * (width // pieces) + j * out_tile, out_tile)
-                cols = pl.ds(first, out_tile)
-                result = jnp.dot(hid[...], wd[:, cols], preferred_element_type=f32)
-                for slot in range(4):
-                    scaled = result[slot * local : (slot + 1) * local] * scales[slot]
-                    part[g, slot, :, cols] = scaled.astype(bf16)
-                return carry
-
-            lax.fori_loop(0, width // pieces // out_tile, out_step, 0)
+            cols = piece_of(p)
+            result = jnp.dot(hid[...], wd[:, cols], preferred_element_type=f32)
+            for slot in range(4):
+                scaled = result[slot * local : (slot + 1) * local] * scales[slot]
+                part[g, slot, :, cols] = scaled.astype(bf16)
             for half in range(2):
                 launch([pair_copy(step, half, p)])
+
+    hidden_total = inner // hidden_tile
+
+    def run_part(step, h):
+        if h == 0:
+            await_sibling(step)
+            if step == 0:
+                for copy in own_copies + weight_copies:
+                    copy.wait()
+        for j in range(hidden_total):
+            if j * (chunks - 1) // hidden_total == h:
+                run_hidden(step, j)
+        if h == chunks - 1:
+            run_out(step)
 
     def pair_sum(g, half, cols):
         return part[g, half * 2 + c, :, cols].astype(f32) + a_in[g, half, :, cols].astype(f32)
@@ -274,18 +294,17 @@
                 c_out[step, :, cols] = acc[...].astype(bf16)
                 launch([chain_copy(step, way, g, p, along(jnp.where(g > z, z + 1, z - 1)))])
 
-    for copy in own_copies:
-        copy.wait()
-    for step in range(depth):
-        if step + 1 < depth:
-            relay_chain(step + 1)
-        relay_across(step)
-        if step == 0:
-            for copy in weight_copies:
-                copy.wait()
-        if step == depth - 1 and depth > 2:
-            send_across(step - 1)
-        run_group(step)
+    for turn in range(1, depth + 1):
+        for h in range(chunks):
+            if turn < depth:
+                relay_chain(turn, h)
+            relay_across(turn - 1, h)
+            if turn >= 2:
+                run_part(turn - 2, h)
+    if depth > 2:
+        send_across(depth - 2)
+    for h in range(chunks):
+        run_part(depth - 1, h)
     order = [depth - 2, depth - 1] + list(range(depth - 3, -1, -1))
     for step in order[1 if depth > 2 else 0 :]:
         send_across(step)
@@ -328,7 +347,7 @@
             pltpu.VMEM((2, depth, local, width), bf16),
             pltpu.VMEM((local, width // pieces), f32),
             dma((3,)), dma((2,)),
-            dma((sends,)), dma((depth, 4)), dma((sends,)), dma((depth, 4)),
+            dma((sends, chunks)), dma((depth, 4, chunks)), dma((sends,)), dma((depth, 4)),
             dma((depth, 2, pieces)), dma((depth, 2, pieces)),
             dma((depth, pieces)), dma((depth, pieces)),
             dma((depth, pieces)), dma((2, depth, pieces)),
@@ -354,7 +373,8 @@
         device_count % 4 == 0
         and device_count >= 8
         and 2 * local_tokens % 128 == 0
-        and model_width % (pieces * out_tile) == 0
+        and local_tokens % (16 * chunks) == 0
+        and model_width % (pieces * 128) == 0
         and inner % hidden_tile == 0
         and 4 * gathered + weights <= vmem_budget
     )

time: 72.7 us -> 65.9 us (0.906)
  Pallas kernels: 69.4 us -> 62.6 us
    pallas_call x1, Pallas kernels: 69.4 us -> 62.6 us  [fused_layer(): pl.pallas_call(functools.partial(fused_kernel, depth), out_shape=jax.Shap...]
where the time goes in v2:
time: 65.9 us; the launch traced here: 65.7 us
  Pallas kernels  62.6 us (95%)
  local copies, waits for them, and re-layouts  1.67 us (3%)
  other arithmetic  1.4 us (2%)
    pallas_call x1, Pallas kernels, fused_layer(): pl.pallas_call(functools.partial(fused_kernel, depth), out_shape=jax.Shap...  62.6 us
    unnamed x1, local copies, waits for them, and re-layouts  1.67 us

profile of v2, /device:TPU:0, one launch (start us, length us, event | category | flops | bytes accessed | tf_op | source)
XLA Modules:
  0.0 65.7 jit_solution(15562176179813597583)
XLA Ops:
  0.0 0.7 %select_reduce_fusion = f32[16,64]{1,0:T(8,128)S(1)} fusion(f32[64,8]{0,1:T(8,128)} %param.8, s32[64,8]{0,1:T(8,128)} %param.7), kind=kLoop, calls=%fused_computation | loop fusion | flops 23552 | bytes 8192 | tf_op jit(solution)/shard_map/reduce_sum | solution.py:364
  0.7 0.7 %pad_maximum_fusion.t_hbm = bf16[16,128]{1,0:T(8,128)(2,1)} fusion(bf16[16,64]{1,0:T(8,128)(2,1)S(1)} %get-tuple-element.6, bf16[16,64]{1,0:T(8,128)(2,1)S(1)} %get-tuple-element.5), kind=kLoop, calls=%fused_computation.5 | loop fusion | flops 8192 | bytes 8192 | tf_op jit(solution)/shard_map/concatenate | solution.py:366
  1.4 62.6 %shard_map.64 = bf16[64,2048]{1,0:T(8,128)(2,1)} custom-call(bf16[64,2048]{1,0:T(8,128)(2,1)} %x_hbm.1, bf16[16,128]{1,0:T(8,128)(2,1)} %pad_maximum_fusion.t_hbm, bf16[1,2048,768]{2,1,0:T(8,128)(2,1)} %wg_hbm.1, bf16[1,2048,768]{2,1,0:T(8,128)(2,1)} %wu_hbm.1, bf16[1,768,2048]{2,1,0:T(8,128)(2,1)} %wd_hbm.1), custom_call_target="tpu_custom_call" | custom-call | tf_op jit(solution)/shard_map/pallas_call | solution.py:330
  64.0 1.7 %copy.10 = bf16[64,2048]{1,0:T(8,128)(2,1)} copy(bf16[64,2048]{1,0:T(8,128)(2,1)} %shard_map.64) | data formatting | bytes 524288
  (1 shorter events, 0.0 us)
